TPU v7x, 32 devices: a whole 2x2x4 slice. The times are simulated.
32 devices in a mesh: prow: 8 (over z, core), pcol: 4 (over y, x).
Axes of the slice: x: 2, y: 2, z: 4, core: 2. Of those that a mesh axis runs over, the one named last changes fastest.
Arguments:
- diag_block: float32 [256, 256], P('prow', 'pcol'), as said below
- panel: float32 [16384, 256], P('prow', 'pcol'), may hold values from -1.5 to 1.5
- slab: float32 [16384, 1024], P('prow', 'pcol'), may hold values from -6 to 6
Outputs:
- diag_factor: float32 [256, 256], P('prow', 'pcol')
- panel_factor: float32 [16384, 256], P('prow', 'pcol')
- slab_updated: float32 [16384, 1024], P('prow', 'pcol')
Inputs may be any that keep to these rules, and one draw needn't show every extreme that they name: diag_block is symmetric positive definite.
All inputs are finite; a program needn't handle non-finite values.
Results may differ from a plain program's by a relative error of at most 0.0003.
Values sent between devices are 32-bit elements; how exact they have to be, the bound alone decides.
A program may use at most 64 MiB of HBM per device.

v0:
```python
import jax
import jax.numpy as jnp
from jax import lax
from jax.sharding import PartitionSpec as P


def broadcast(block, axis, source):
    block = jnp.where(lax.axis_index(axis) == source, block, jnp.zeros_like(block))
    return lax.psum(block, axis)


def local(diag_block, panel, slab):
    row_count = lax.axis_size("prow")
    col_count = lax.axis_size("pcol")
    row_index = lax.axis_index("prow")
    col_index = lax.axis_index("pcol")
    diag_tile = lax.all_gather(diag_block, "pcol", axis=1, tiled=True)
    full_block = lax.all_gather(diag_tile, "prow", axis=0, tiled=True)
    diag_factor = jnp.linalg.cholesky(full_block)
    block_size = full_block.shape[0]
    col_width = panel.shape[1]
    local_rows = panel.shape[0]
    blocks_here = local_rows // block_size
    group = blocks_here * row_count // col_count
    full_rows = lax.all_gather(panel, "pcol", axis=1, tiled=True)
    inverse = jax.scipy.linalg.solve_triangular(
        diag_factor, jnp.eye(block_size, dtype=jnp.float32), lower=True
    )
    factor = jnp.dot(
        full_rows, inverse.T, precision=lax.Precision.HIGHEST, preferred_element_type=jnp.float32
    )
    diag_out = lax.dynamic_slice(
        diag_factor,
        (row_index * diag_block.shape[0], col_index * diag_block.shape[1]),
        (diag_block.shape[0], diag_block.shape[1]),
    )
    panel_out = lax.dynamic_slice_in_dim(factor, col_index * col_width, col_width, 1)
    target = col_index * group
    root_row = target % row_count
    local_block = target // row_count
    chosen = lax.dynamic_slice_in_dim(factor, local_block * block_size, block_size, 0)
    remote = broadcast(chosen, "prow", root_row)
    product = jnp.dot(
        factor, remote.T, precision=lax.Precision.HIGHEST, preferred_element_type=jnp.float32
    )
    position = jnp.arange(local_rows, dtype=jnp.int32)
    row_global = (
        position // block_size * row_count + row_index
    ) * block_size + position % block_size
    col_global = target * block_size + jnp.arange(block_size, dtype=jnp.int32)
    keep_mask = row_global[:, None] >= col_global[None, :]
    updated = jnp.where(keep_mask, slab - product, slab)
    return (diag_out, panel_out, updated)


def solution(mesh):
    placed = (P("prow", "pcol"), P("prow", "pcol"), P("prow", "pcol"))
    return jax.shard_map(
        local,
        mesh=mesh,
        in_specs=placed,
        out_specs=(P("prow", "pcol"), P("prow", "pcol"), P("prow", "pcol")),
        check_vma=False,
    )
```

profile of v0, /device:TPU:0, one launch (start us, length us, event | category | flops | bytes accessed | tf_op | source)
XLA Modules:
  0.0 166.8 jit_solution(1090098768620998737)
XLA Ops:
  7.2 0.0 all-gather.3.cloned.1.call-start
  7.2 0.7 all-gather.3.cloned.1.call-update
  7.9 0.0 all-reduce.3.cloned.1.call-start
  8.0 9.9 %all-gather = f32[4,64,32]{1,2,0:T(8,128)S(1)} all-gather(f32[1,64,32]{1,2,0:T(8,128)} %bitcast.45), channel_id=1, replica_groups=mesh['prow'=8,'pcol'=4] {'pcol'}, dimensions={0}, use_global_device_ids=true | all-gather | bytes 40960 | tf_op jit(solution)/shard_map/all_gather | solution.py:17
  17.9 0.1 reshape.73
  18.0 14.4 %all_gather.10 = f32[256,256]{1,0:T(8,128)S(1)} all-gather(f32[32,256]{1,0:T(8,128)S(1)} %bitcast.44), channel_id=1, replica_groups=mesh['prow'=8,'pcol'=4] {'prow'}, dimensions={0}, use_global_device_ids=true | all-gather | bytes 294912 | tf_op jit(solution)/shard_map/all_gather | solution.py:18
  32.4 0.1 copy.10
  32.6 11.7 %cholesky.50 = f32[128,128]{1,0:T(8,128)S(1)} custom-call(f32[128,128]{1,0:T(8,128)S(1)} %cholesky.118), custom_call_target="Cholesky" | custom-call | tf_op jit(solution)/shard_map/jit(cholesky)/cholesky | solution.py:19
  44.4 9.8 %custom-call.15 = f32[1,128,128]{1,2,0:T(8,128)S(1)} custom-call(f32[1,128,128]{2,1,0:T(8,128)S(1)} %get-tuple-element.26), custom_call_target="InvertDiagBlocksLowerTriangular" | custom-call | tf_op jit(solution)/shard_map/jit(cholesky)/cholesky | solution.py:19
  54.2 0.2 constant_dynamic-update-slice_fusion
  54.4 0.3 convolution_subtract_fusion.1
  54.7 11.7 %cholesky.105 = f32[128,128]{1,0:T(8,128)S(1)} custom-call(f32[128,128]{1,0:T(8,128)S(1)} %convolution_subtract_fusion.1), custom_call_target="Cholesky" | custom-call | tf_op jit(solution)/shard_map/jit(cholesky)/cholesky | solution.py:19
  66.4 0.6 compare_reduce_fusion
  68.4 0.1 triangular_solve.44
  68.5 4.1 %while.1 = (s32[]{:T(128)}, f32[256,256]{1,0:T(8,128)S(1)}, s32[2,2]{1,0:T(2,128)S(1)}, f32[2,128,128]{2,1,0:T(8,128)S(1)}, s32[]{:T(128)}) while((s32[]{:T(128)}, f32[256,256]{1,0:T(8,128)S(1)}, s32[2,2]{1,0:T(2,128)S(1)}, f32[2,128,128]{2,1,0:T(8,128)S(1)}, s32[]{:T(128)}) %tuple.28), condition=%wide.while_cond, body=%wide.while_body.sunk | while | flops 2 | bytes 131181 | solution.py:26
  68.7 0.6 fusion.34
  69.3 1.4 bitcast_dynamic-update-slice_fusion.2
  70.7 0.6 fusion.34
  71.3 1.4 bitcast_dynamic-update-slice_fusion.2
  72.7 19.7 %custom-call.16 = f32[2,128,128]{1,2,0:T(8,128)S(1)} custom-call(f32[2,128,128]{2,1,0:T(8,128)S(1)} %get-tuple-element.10), custom_call_target="InvertDiagBlocksLowerTriangular" | custom-call | tf_op jit(solution)/shard_map/jit(_solve_triangular)/triangular_solve | solution.py:26
  92.4 0.7 dynamic_slice.9
  93.1 0.3 fusion.6
  93.4 0.3 convolution_subtract_fusion
  93.7 0.3 fusion.9
  94.0 0.0 all-gather.3.cloned.1.call-done
  94.0 3.5 %fusion = f32[256,2048]{1,0:T(8,128)S(1)} fusion(f32[2048,256]{0,1:T(8,128)} %all-gather.3.cloned.1.call-done, f32[128,256]{1,0:T(8,128)S(1)} %fusion.9, f32[128,256]{1,0:T(8,128)S(1)} %fusion.6), kind=kOutput, calls=%fused_computation.6 | convolution fusion | flops 1610678272 | bytes 4456448 | tf_op jit(solution)/shard_map/dot_general | solution.py:29
  97.5 0.7 select_bitcast_fusion
  98.2 0.0 all-reduce.3.cloned.1.call-update
  98.2 0.8 dynamic-slice_bitcast_fusion
  99.1 54.8 %all-reduce.3.cloned.1.call-done = f32[256,256]{0,1:T(8,128)} async-done(((f32[256,256]{0,1:T(8,128)}), f32[256,256]{0,1:T(8,128)}) %all-reduce.3.cloned.1.call-update) | async-done | bytes 262160 | tf_op jit(solution)/shard_map/psum | solution.py:9
  153.9 6.1 %subtract_select_fusion = f32[2048,256]{1,0:T(8,128)} fusion(f32[2048,256]{1,0:T(8,128)} %param.5, f32[256,2048]{1,0:T(8,128)S(1)} %fusion, f32[256,256]{0,1:T(8,128)} %all-reduce.3.cloned.1.call-done, s32[256]{0:T(256)S(1)} %iota_add_fusion, s32[2048]{0:T(1024)S(1)} %fusion.22), kind=kOutput, calls=%fused_computation.2 | convolution fusion | flops 1612185600 | bytes 6562816 | tf_op jit(solution)/shard_map/dot_general | solution.py:43
  (14 shorter events, 0.3 us)
Async XLA Ops:
  7.2 86.8 %all-gather.3.cloned.1.call-start = ((), (), s32[]{:S(2)}) async-start(), calls=%async_computation | async-start | bytes 2621440 | tf_op jit(solution)/shard_map/all_gather | solution.py:25
  7.9 146.0 %all-reduce.3.cloned.1.call-start = ((), (), s32[]{:S(2)}) async-start(), calls=%async_computation.1 | async-start | bytes 524288 | tf_op jit(solution)/shard_map/psum | solution.py:9
Sparse Core Ops, SparseCore 0:
  9.8 37.9 all-gather.2
  98.3 55.4 all-reduce.2
where the time goes:
time: 167 us
  waiting for transfers between devices  55.5 us (33%)
  other arithmetic  54.5 us (33%)
  blocking collectives  24.3 us (15%)
  between operations  15.5 us (9%)
  matrix products  10.9 us (7%)
  local copies, waits for them, and re-layouts  5.85 us (4%)
    psum x1, waiting for transfers between devices, broadcast(): return lax.psum(block, axis)  54.8 us
    another operation x6, other arithmetic, local(): diag_factor = jnp.linalg.cholesky(full_block)  34 us
    another operation x3, other arithmetic, local(): jax.scipy.linalg.solve_triangular(diag_factor, jnp.eye(block_size, dtype=...  19.7 us
    all_gather x1, blocking collectives, local(): full_block = lax.all_gather(diag_tile, 'prow', axis=0, tiled=True)  14.4 us
    all_gather x1, blocking collectives, local(): diag_tile = lax.all_gather(diag_block, 'pcol', axis=1, tiled=True)  9.88 us
    dot_general x1, matrix products, local(): jnp.dot(factor, remote.T, precision=lax.Precision.HIGHEST, preferred_elem...  6.11 us
    another operation x6, local copies, waits for them, and re-layouts  3.95 us
    dot_general x1, matrix products, local(): jnp.dot(full_rows, inverse.T, precision=lax.Precision.HIGHEST, preferred_...  3.47 us
  transfers between devices with their start and end apart: 2, of which 1 were waited for; matrix products, arithmetic and copies ran while one was open for 37% of the time, Pallas kernels for 0%

commit v1 on v0

--- a/solution.py
+++ b/solution.py
@@ -15,7 +15,25 @@
     row_index = lax.axis_index("prow")
     col_index = lax.axis_index("pcol")
     diag_tile = lax.all_gather(diag_block, "pcol", axis=1, tiled=True)
-    full_block = lax.all_gather(diag_tile, "prow", axis=0, tiled=True)
+    count, position_2, rows = (lax.axis_size("prow"), lax.axis_index("prow"), diag_tile.shape[0])
+    ahead = [(i, (i + 1) % count) for i in range(count)]
+    left = [(i, (i - 1) % count) for i in range(count)]
+    full_block = jnp.zeros(
+        (*diag_tile.shape[:0], count * rows, *diag_tile.shape[0 + 1 :]), diag_tile.dtype
+    )
+    full_block = lax.dynamic_update_slice_in_dim(full_block, diag_tile, position_2 * rows, axis=0)
+    from_left = from_right = diag_tile
+    half = count // 2
+    for step in range(1, half + 1):
+        from_left = lax.ppermute(from_left, "prow", ahead)
+        full_block = lax.dynamic_update_slice_in_dim(
+            full_block, from_left, (position_2 - step) % count * rows, axis=0
+        )
+        if step < count - half:
+            from_right = lax.ppermute(from_right, "prow", left)
+            full_block = lax.dynamic_update_slice_in_dim(
+                full_block, from_right, (position_2 + step) % count * rows, axis=0
+            )
     diag_factor = jnp.linalg.cholesky(full_block)
     block_size = full_block.shape[0]
     col_width = panel.shape[1]

time: 167 us -> 182 us (1.090)
  blocking collectives: 24.3 us -> 9.88 us
  starting transfers between devices: 0.08 us -> 11.1 us
  local copies, waits for them, and re-layouts: 5.85 us -> 15.1 us
  waiting for transfers between devices: 55.5 us -> 63.9 us
    all_gather x1 -> x0, blocking collectives: 14.4 us -> none  [local(): full_block = lax.all_gather(diag_tile, 'prow', axis=0, tiled=True)]
    ppermute x0 -> x7, starting transfers between devices: none -> 11 us  [the longest x3 10.9 us: local(): from_right = lax.ppermute(from_right, 'prow', left)]
    ppermute x0 -> x7, waiting for transfers between devices: none -> 8.9 us  [the longest x4 8.84 us: local(): from_left = lax.ppermute(from_left, 'prow', ahead)]
    dynamic_update_slice x0 -> x9, local copies, waits for them, and re-layouts: none -> 8.69 us  [the longest x3 4 us: local(): lax.dynamic_update_slice_in_dim(full_block, from_right, (position_2 + ste...]
    another operation x6 -> x11, local copies, waits for them, and re-layouts: 3.95 us -> 4.17 us
  transfers between devices with their start and end apart: 2 -> 9, of which waited for: 1 -> 5; matrix products, arithmetic and copies ran while one was open for 37% -> 39% of each run, Pallas kernels for 0% -> 0%
where the time goes in v1:
time: 182 us; the launch traced here: 181 us
  waiting for transfers between devices  63.9 us (35%)
  other arithmetic  54.7 us (30%)
  between operations  15.7 us (9%)
  local copies, waits for them, and re-layouts  15.1 us (8%)
  starting transfers between devices  11.1 us (6%)
  matrix products  10.9 us (6%)
  blocking collectives  9.88 us (5%)
    psum x1, waiting for transfers between devices, broadcast(): return lax.psum(block, axis)  55 us
    another operation x6, other arithmetic, local(): diag_factor = jnp.linalg.cholesky(full_block)  33.9 us
    another operation x3, other arithmetic, local(): jax.scipy.linalg.solve_triangular(diag_factor, jnp.eye(block_size, dtype=...  19.9 us
    ppermute x3, starting transfers between devices, local(): from_right = lax.ppermute(from_right, 'prow', left)  10.9 us
    all_gather x1, blocking collectives, local(): diag_tile = lax.all_gather(diag_block, 'pcol', axis=1, tiled=True)  9.88 us
    ppermute x4, waiting for transfers between devices, local(): from_left = lax.ppermute(from_left, 'prow', ahead)  8.84 us
    dot_general x1, matrix products, local(): jnp.dot(factor, remote.T, precision=lax.Precision.HIGHEST, preferred_elem...  6.1 us
    another operation x11, local copies, waits for them, and re-layouts  4.17 us
  transfers between devices with their start and end apart: 9, of which 5 were waited for; matrix products, arithmetic and copies ran while one was open for 39% of the time, Pallas kernels for 0%

profile of v1, /device:TPU:0, one launch (start us, length us, event | category | flops | bytes accessed | tf_op | source)
XLA Modules:
  0.0 181.3 jit_solution(9311461919702681612)
XLA Ops:
  7.2 9.9 %all-gather = f32[4,64,32]{1,2,0:T(8,128)S(1)} all-gather(f32[1,64,32]{1,2,0:T(8,128)} %bitcast.45), channel_id=1, replica_groups=mesh['prow'=8,'pcol'=4] {'pcol'}, dimensions={0}, use_global_device_ids=true | all-gather | bytes 40960 | tf_op jit(solution)/shard_map/all_gather | solution.py:17
  17.1 0.1 copy.14
  17.2 0.1 collective-permute-start
  17.3 3.5 %collective-permute-start.1 = (f32[32,256]{0,1:T(8,128)S(1)}, f32[32,256]{0,1:T(8,128)S(1)}, u32[]{:S(2)}, u32[]{:S(2)}) collective-permute-start(f32[32,256]{0,1:T(8,128)S(1)} %bitcast.43), channel_id=1, source_target_pairs={{0,28},{4,0},{8,4},{12,8},{16,12},{20,16},{24,20},{28,24},{1,29},{... | collective-permute-start | bytes 98312 | tf_op jit(solution)/shard_map/ppermute | solution.py:33
  20.9 2.6 %collective-permute-done = f32[32,256]{0,1:T(8,128)S(1)} collective-permute-done((f32[32,256]{0,1:T(8,128)S(1)}, f32[32,256]{0,1:T(8,128)S(1)}, u32[]{:S(2)}, u32[]{:S(2)}) %collective-permute-start) | collective-permute-done | bytes 32800 | tf_op jit(solution)/shard_map/ppermute | solution.py:28
  23.6 3.6 %collective-permute-start.3 = (f32[32,256]{0,1:T(8,128)S(1)}, f32[32,256]{0,1:T(8,128)S(1)}, u32[]{:S(2)}, u32[]{:S(2)}) collective-permute-start(f32[32,256]{0,1:T(8,128)S(1)} %collective-permute-done.1), channel_id=1, source_target_pairs={{0,28},{4,0},{8,4},{12,8},{16,12},{20,16},{24,20},{28,24},{1,29},{... | collective-permute-start | bytes 98312 | tf_op jit(solution)/shard_map/ppermute | solution.py:33
  27.1 3.7 %collective-permute-done.2 = f32[32,256]{0,1:T(8,128)S(1)} collective-permute-done((f32[32,256]{0,1:T(8,128)S(1)}, f32[32,256]{0,1:T(8,128)S(1)}, u32[]{:S(2)}, u32[]{:S(2)}) %collective-permute-start.2) | collective-permute-done | bytes 32800 | tf_op jit(solution)/shard_map/ppermute | solution.py:28
  30.9 0.1 collective-permute-done.3
  30.9 3.8 %collective-permute-start.5 = (f32[32,256]{0,1:T(8,128)S(1)}, f32[32,256]{0,1:T(8,128)S(1)}, u32[]{:S(2)}, u32[]{:S(2)}) collective-permute-start(f32[32,256]{0,1:T(8,128)S(1)} %collective-permute-done.3), channel_id=1, source_target_pairs={{0,28},{4,0},{8,4},{12,8},{16,12},{20,16},{24,20},{28,24},{1,29},{... | collective-permute-start | bytes 98312 | tf_op jit(solution)/shard_map/ppermute | solution.py:33
  34.7 2.5 %collective-permute-done.4 = f32[32,256]{0,1:T(8,128)S(1)} collective-permute-done((f32[32,256]{0,1:T(8,128)S(1)}, f32[32,256]{0,1:T(8,128)S(1)}, u32[]{:S(2)}, u32[]{:S(2)}) %collective-permute-start.4) | collective-permute-done | bytes 32800 | tf_op jit(solution)/shard_map/ppermute | solution.py:28
  37.3 1.1 dynamic_update_slice.24
  38.4 0.9 dynamic_update_slice.25
  39.3 1.3 dynamic_update_slice.26
  40.6 0.9 dynamic_update_slice.27
  41.5 1.3 dynamic_update_slice.28
  42.9 0.9 dynamic_update_slice.29
  43.8 1.3 dynamic_update_slice.30
  45.1 0.8 dynamic_update_slice.31
  45.9 0.1 copy.15
  46.1 11.7 %cholesky.49 = f32[128,128]{1,0:T(8,128)S(1)} custom-call(f32[128,128]{1,0:T(8,128)S(1)} %cholesky.115), custom_call_target="Cholesky" | custom-call | tf_op jit(solution)/shard_map/jit(cholesky)/cholesky | solution.py:37
  57.8 0.1 copy.16
  58.0 9.8 %custom-call.15 = f32[1,128,128]{1,2,0:T(8,128)S(1)} custom-call(f32[1,128,128]{2,1,0:T(8,128)S(1)} %get-tuple-element.38), custom_call_target="InvertDiagBlocksLowerTriangular" | custom-call | tf_op jit(solution)/shard_map/jit(cholesky)/cholesky | solution.py:37
  67.8 0.2 fusion.10
  68.0 0.1 copy.17
  68.1 0.3 slice_subtract_fusion
  68.4 11.7 %cholesky.103 = f32[128,128]{1,0:T(8,128)S(1)} custom-call(f32[128,128]{1,0:T(8,128)S(1)} %slice_subtract_fusion), custom_call_target="Cholesky" | custom-call | tf_op jit(solution)/shard_map/jit(cholesky)/cholesky | solution.py:37
  80.1 0.1 copy.18
  80.3 0.6 compare_reduce_fusion
  82.3 0.1 triangular_solve.44
  82.4 4.2 %while.1 = (s32[]{:T(128)}, f32[256,256]{0,1:T(8,128)S(1)}, s32[2,2]{1,0:T(2,128)S(1)}, f32[2,128,128]{2,1,0:T(8,128)S(1)}, s32[]{:T(128)}) while((s32[]{:T(128)}, f32[256,256]{0,1:T(8,128)S(1)}, s32[2,2]{1,0:T(2,128)S(1)}, f32[2,128,128]{2,1,0:T(8,128)S(1)}, s32[]{:T(128)}) %tuple.30), condition=%wide.while_cond, body=%wide.while_body.sunk | while | flops 2 | bytes 393321 | solution.py:44
  82.4 0.6 fusion.34
  83.0 1.4 dynamic-slice.13
  84.3 0.1 copy.25
  84.5 0.6 fusion.34
  85.1 1.4 dynamic-slice.13
  86.5 0.1 copy.25
  86.6 19.9 %custom-call.16 = f32[2,128,128]{1,2,0:T(8,128)S(1)} custom-call(f32[2,128,128]{2,1,0:T(8,128)S(1)} %get-tuple-element.10), custom_call_target="InvertDiagBlocksLowerTriangular" | custom-call | tf_op jit(solution)/shard_map/jit(_solve_triangular)/triangular_solve | solution.py:44
  106.5 0.1 dynamic_slice.9
  106.6 0.7 copy.21
  107.3 0.3 fusion.6
  107.5 0.3 convolution_subtract_fusion
  107.8 0.3 fusion.9
  108.2 3.5 %fusion = f32[256,2048]{1,0:T(8,128)S(1)} fusion(f32[2048,256]{0,1:T(8,128)} %all-gather.3.cloned.1.call-done, f32[128,256]{1,0:T(8,128)S(1)} %fusion.9, f32[128,256]{1,0:T(8,128)S(1)} %fusion.6), kind=kOutput, calls=%fused_computation.5 | convolution fusion | flops 1610678272 | bytes 4456448 | tf_op jit(solution)/shard_map/dot_general | solution.py:47
  111.7 0.1 copy.23
  111.8 0.7 select_bitcast_fusion
  112.6 0.8 dynamic-slice_bitcast_fusion
  113.4 55.0 %all-reduce.3.cloned.1.call-done = f32[256,256]{1,0:T(8,128)} async-done(((f32[256,256]{1,0:T(8,128)}), f32[256,256]{1,0:T(8,128)}) %all-reduce.3.cloned.1.call-update) | async-done | bytes 262160 | tf_op jit(solution)/shard_map/psum | solution.py:9
  168.4 6.1 %subtract_select_fusion = f32[2048,256]{1,0:T(8,128)} fusion(f32[2048,256]{1,0:T(8,128)} %param.5, f32[256,2048]{1,0:T(8,128)S(1)} %fusion, f32[256,256]{1,0:T(8,128)} %all-reduce.3.cloned.1.call-done, s32[256]{0:T(256)S(1)} %iota_add_fusion, s32[2048]{0:T(1024)S(1)} %fusion.22), kind=kOutput, calls=%fused_computation.2 | convolution fusion | flops 1612185600 | bytes 6562816 | tf_op jit(solution)/shard_map/dot_general | solution.py:61
  (30 shorter events, 0.5 us)
Async XLA Ops:
  7.2 101.0 %all-gather.3.cloned.1.call-start = ((), (), s32[]{:S(2)}) async-start(), calls=%async_computation | async-start | bytes 2621440 | tf_op jit(solution)/shard_map/all_gather | solution.py:43
  17.2 6.3 %collective-permute-start = (f32[32,256]{0,1:T(8,128)S(1)}, f32[32,256]{0,1:T(8,128)S(1)}, u32[]{:S(2)}, u32[]{:S(2)}) collective-permute-start(f32[32,256]{0,1:T(8,128)S(1)} %bitcast.42), channel_id=1, source_target_pairs={{0,4},{4,8},{8,12},{12,16},{16,20},{20,24},{24,28},{28,0},{1,5},{5... | collective-permute-start | bytes 98312 | tf_op jit(solution)/shard_map/ppermute | solution.py:28
  17.3 6.3 %collective-permute-start.1 = (f32[32,256]{0,1:T(8,128)S(1)}, f32[32,256]{0,1:T(8,128)S(1)}, u32[]{:S(2)}, u32[]{:S(2)}) collective-permute-start(f32[32,256]{0,1:T(8,128)S(1)} %bitcast.43), channel_id=1, source_target_pairs={{0,28},{4,0},{8,4},{12,8},{16,12},{20,16},{24,20},{28,24},{1,29},{... | collective-permute-start | bytes 98312 | tf_op jit(solution)/shard_map/ppermute | solution.py:33
  20.8 147.6 %all-reduce.3.cloned.1.call-start = ((), (), s32[]{:S(2)}) async-start(), calls=%async_computation.1 | async-start | bytes 524288 | tf_op jit(solution)/shard_map/psum | solution.py:9
  23.5 7.3 %collective-permute-start.2 = (f32[32,256]{0,1:T(8,128)S(1)}, f32[32,256]{0,1:T(8,128)S(1)}, u32[]{:S(2)}, u32[]{:S(2)}) collective-permute-start(f32[32,256]{0,1:T(8,128)S(1)} %collective-permute-done), channel_id=1, source_target_pairs={{0,4},{4,8},{8,12},{12,16},{16,20},{20,24},{24,28},{28,0},{1,5},{5... | collective-permute-start | bytes 98312 | tf_op jit(solution)/shard_map/ppermute | solution.py:28
  23.6 7.4 %collective-permute-start.3 = (f32[32,256]{0,1:T(8,128)S(1)}, f32[32,256]{0,1:T(8,128)S(1)}, u32[]{:S(2)}, u32[]{:S(2)}) collective-permute-start(f32[32,256]{0,1:T(8,128)S(1)} %collective-permute-done.1), channel_id=1, source_target_pairs={{0,28},{4,0},{8,4},{12,8},{16,12},{20,16},{24,20},{28,24},{1,29},{... | collective-permute-start | bytes 98312 | tf_op jit(solution)/shard_map/ppermute | solution.py:33
  30.9 6.4 %collective-permute-start.4 = (f32[32,256]{0,1:T(8,128)S(1)}, f32[32,256]{0,1:T(8,128)S(1)}, u32[]{:S(2)}, u32[]{:S(2)}) collective-permute-start(f32[32,256]{0,1:T(8,128)S(1)} %collective-permute-done.2), channel_id=1, source_target_pairs={{0,4},{4,8},{8,12},{12,16},{16,20},{20,24},{24,28},{28,0},{1,5},{5... | collective-permute-start | bytes 98312 | tf_op jit(solution)/shard_map/ppermute | solution.py:28
  30.9 12.8 %collective-permute-start.5 = (f32[32,256]{0,1:T(8,128)S(1)}, f32[32,256]{0,1:T(8,128)S(1)}, u32[]{:S(2)}, u32[]{:S(2)}) collective-permute-start(f32[32,256]{0,1:T(8,128)S(1)} %collective-permute-done.3), channel_id=1, source_target_pairs={{0,28},{4,0},{8,4},{12,8},{16,12},{20,16},{24,20},{28,24},{1,29},{... | collective-permute-start | bytes 98312 | tf_op jit(solution)/shard_map/ppermute | solution.py:33
  37.2 7.9 %collective-permute-start.6 = (f32[32,256]{0,1:T(8,128)S(1)}, f32[32,256]{0,1:T(8,128)S(1)}, u32[]{:S(2)}, u32[]{:S(2)}) collective-permute-start(f32[32,256]{0,1:T(8,128)S(1)} %collective-permute-done.4), channel_id=1, source_target_pairs={{0,4},{4,8},{8,12},{12,16},{16,20},{20,24},{24,28},{28,0},{1,5},{5... | collective-permute-start | bytes 98312 | tf_op jit(solution)/shard_map/ppermute | solution.py:28
Sparse Core Ops, SparseCore 0:
  20.9 33.6 all-gather.2
  112.7 55.6 all-reduce.2
